TPU v7x, 32 devices: a whole 2x2x4 slice. The times are simulated.
32 devices in a mesh: row: 8 (over z, core), col: 4 (over y, x).
Axes of the slice: x: 2, y: 2, z: 4, core: 2. Of those that a mesh axis runs over, the one named last changes fastest.
Arguments:
- context: bfloat16 [128, 16384], P('row', 'col'), may hold values from -6 to 6
- out_weight: bfloat16 [16384, 16384], P('col', 'row'), may hold values from -0.046875 to 0.046875
- residual: bfloat16 [128, 16384], P('col', 'row'), may hold values from -80 to 80
- teacher_gain: float32 [16384], replicated, may hold values from 0.5 to 1.5
- student_hidden: bfloat16 [128, 4096], P(('row', 'col')), may hold values from -6 to 6
- student_gain: float32 [4096], replicated, may hold values from 0.5 to 1.5
- projector: bfloat16 [4096, 16384], P(None, ('row', 'col')), may hold values from -0.09375 to 0.09375
Outputs:
- grad_proj: float32 [4096, 16384], P(None, ('row', 'col'))
- grad_gain: float32 [4096], replicated
- loss: float32 [], replicated
All inputs are finite; a program needn't handle non-finite values.
Results may differ from a plain program's by a relative error of at most 0.0065.
Values may be sent and summed in bfloat16 or wider, within the bound.
A program may use at most 64 MiB of HBM per device.

v0:
```python
import jax
import jax.numpy as jnp
from jax import lax
from jax.sharding import PartitionSpec as P

D_T = 16384
norm_eps = 1e-05


def normalize(hidden):
    widened = hidden.astype(jnp.float32)
    return widened * lax.rsqrt(jnp.mean(widened * widened, axis=1, keepdims=True) + norm_eps)


def per_device(
    context, out_weight, residual, teacher_gain, student_hidden, student_gain, projector
):
    row_index = lax.axis_index("row")
    context_all = lax.all_gather(context, "row", axis=0, tiled=True)
    out_block = out_weight.shape[1]
    summed = lax.psum_scatter(
        jnp.dot(context_all, out_weight, preferred_element_type=jnp.float32),
        "col",
        scatter_dimension=0,
        tiled=True,
    )
    summed = summed + residual.astype(jnp.float32)
    squares = lax.psum(jnp.sum(summed * summed, axis=1), "row")
    gain_block = lax.dynamic_slice_in_dim(teacher_gain, row_index * out_block, out_block)
    final_rows = (summed * lax.rsqrt(squares / D_T + norm_eps)[:, None] * gain_block).astype(
        jnp.bfloat16
    )
    target = lax.all_to_all(final_rows, "col", split_axis=1, concat_axis=0, tiled=True)
    hidden_all = lax.all_gather(student_hidden, ("row", "col"), axis=0, tiled=True)
    normed_all = normalize(hidden_all)
    student_all = (normed_all * student_gain).astype(jnp.bfloat16)
    predicted = jnp.dot(student_all, projector, preferred_element_type=jnp.float32)
    difference = predicted - target.astype(jnp.float32)
    loss_part = jnp.sum(difference * difference)
    loss_total = lax.psum(loss_part, ("row", "col"))
    error_term = (difference * (1.0 / 64.0)).astype(jnp.bfloat16)
    grad_proj = lax.dot_general(
        student_all, error_term, (((0,), (0,)), ((), ())), preferred_element_type=jnp.float32
    )
    grad_normed = lax.dot_general(
        error_term, projector, (((1,), (1,)), ((), ())), preferred_element_type=jnp.float32
    )
    gain_part = jnp.sum(grad_normed * normed_all, axis=0)
    grad_gain = lax.psum(gain_part, ("row", "col"))
    tokens_all = predicted.shape[0]
    loss = loss_total / (tokens_all * D_T)
    return (grad_proj, grad_gain, loss)


def solution(mesh):
    placed = (
        P("row", "col"),
        P("col", "row"),
        P("col", "row"),
        P(),
        P(("row", "col"), None),
        P(),
        P(None, ("row", "col")),
    )
    return jax.shard_map(
        per_device,
        mesh=mesh,
        in_specs=placed,
        out_specs=(P(None, ("row", "col")), P(), P()),
        check_vma=False,
    )
```

profile of v0, /device:TPU:12, one launch (start us, length us, event | category | flops | bytes accessed | tf_op | source)
XLA Modules:
  0.0 205.2 jit_solution(2190091404144003150)
XLA Ops:
  7.2 0.0 all-gather.4.cloned.1.call-start
  7.2 0.7 all-gather.4.cloned.1.call-update
  7.9 0.0 all-gather.6.cloned.1.call-start
  7.9 0.7 all-gather.6.cloned.1.call-update
  8.6 0.0 reduce-scatter.2.cloned.1.call-start
  8.7 24.4 %all-gather.4.cloned.1.call-done = bf16[128,4096]{1,0:T(8,128)(2,1)} async-done(((bf16[16,4096]{1,0:T(8,128)(2,1)}), bf16[128,4096]{1,0:T(8,128)(2,1)}) %all-gather.4.cloned.1.call-update) | async-done | bytes 1048592 | tf_op jit(solution)/shard_map/all_gather | solution.py:19
  33.1 9.4 %fusion.4 = f32[128,2048]{1,0:T(8,128)} fusion(bf16[128,4096]{1,0:T(8,128)(2,1)} %all-gather.4.cloned.1.call-done, bf16[4096,2048]{1,0:T(8,128)(2,1)} %param.8), kind=kOutput, calls=%fused_computation.16 | convolution fusion | flops 2147483648 | bytes 18874368 | tf_op jit(solution)/shard_map/dot_general | solution.py:22
  42.5 0.0 reduce-scatter.2.cloned.1.call-update
  42.5 0.0 copy-start.1
  42.5 0.0 dynamic-slice-start
  42.5 46.0 %all-gather.6.cloned.1.call-done = bf16[32,4,4096]{2,1,0:T(4,128)(2,1)} async-done(((bf16[1,4,4096]{2,1,0:T(4,128)(2,1)}), bf16[32,4,4096]{2,1,0:T(4,128)(2,1)}) %all-gather.6.cloned.1.call-update) | async-done | bytes 1048592 | tf_op jit(solution)/shard_map/all_gather | solution.py:34
  88.5 1.3 reshape.25
  89.8 0.2 multiply_reduce_fusion
  90.0 29.6 %reduce-scatter.2.cloned.1.call-done = f32[32,2048]{1,0:T(8,128)} async-done(((f32[128,2048]{1,0:T(8,128)}), f32[32,2048]{1,0:T(8,128)}) %reduce-scatter.2.cloned.1.call-update) | async-done | bytes 262160 | tf_op jit(solution)/shard_map/reduce_scatter | solution.py:21
  119.7 1.1 multiply_reduce_fusion.2
  120.8 12.7 %psum.21 = f32[32]{0:T(128)S(1)} all-reduce(f32[32]{0:T(128)S(1)} %multiply_reduce_fusion.2), channel_id=1, replica_groups=mesh['row'=8,'col'=4] {'row'}, use_global_device_ids=true, to_apply=%region_3.0 | all-reduce | flops 32 | bytes 256 | tf_op jit(solution)/shard_map/psum | solution.py:28
  133.4 1.0 multiply_convert_fusion.2
  134.5 0.7 copy.14
  135.2 3.9 %all-to-all-start = ((bf16[32,4,512]{2,0,1:T(8,128)(2,1)}), bf16[32,4,512]{2,0,1:T(8,128)(2,1)S(1)}, u32[]{:S(2)}, u32[]{:S(2)}) async-start(bf16[32,4,512]{2,0,1:T(8,128)(2,1)} %bitcast.11), calls=%async_computation.1 | async-start | bytes 262144 | tf_op jit(solution)/shard_map/all_to_all | solution.py:33
  139.0 3.9 %all-to-all-done = bf16[32,4,512]{2,0,1:T(8,128)(2,1)S(1)} async-done(((bf16[32,4,512]{2,0,1:T(8,128)(2,1)}), bf16[32,4,512]{2,0,1:T(8,128)(2,1)S(1)}, u32[]{:S(2)}, u32[]{:S(2)}) %all-to-all-start) | async-done | bytes 131104 | tf_op jit(solution)/shard_map/all_to_all | solution.py:33
  143.0 3.7 %multiply_reduce_fusion.1 = (f32[]{:T(128)}, f32[128,512]{1,0:T(8,128)S(1)}) fusion(f32[128,512]{1,0:T(8,128)S(1)} %bitcast.12, bf16[4096,512]{1,0:T(8,128)(2,1)} %param.13, f32[128,4096]{1,0:T(8,128)S(1)} %reshape.25, f32[4096]{0:T(1024)S(1)} %copy-done.2, f32[128]{0:T(128)S(1)} %add_rsqrt_fusion.1), kind=kOutput, calls=%fused_computation.5 | convolution fusion | flops 538640384 | bytes 6832644 | tf_op jit(solution)/shard_map/dot_general | solution.py:37
  146.7 1.5 fusion
  148.2 4.8 %fusion.1 = f32[4096,512]{1,0:T(8,128)} fusion(f32[128,512]{1,0:T(8,128)S(1)} %get-tuple-element.6, f32[128,4096]{1,0:T(8,128)S(1)} %reshape.25, f32[4096]{0:T(1024)S(1)} %copy-done.2, f32[128]{0:T(128)S(1)} %add_rsqrt_fusion.1), kind=kOutput, calls=%fused_computation.11 | convolution fusion | flops 538574848 | bytes 10764800 | tf_op jit(solution)/shard_map/dot_general | solution.py:42
  153.0 43.9 %all-reduce = (f32[4096]{0:T(1024)}, f32[]{:T(128)}) all-reduce(f32[4096]{0:T(1024)S(1)} %fusion, f32[]{:T(128)} %get-tuple-element.5), channel_id=1, replica_groups=mesh['row'=8,'col'=4] {'row','col'}, use_global_device_ids=true, to_apply=%region_5.0 | all-reduce | flops 4097 | bytes 32776 | tf_op jit(solution)/shard_map/psum | solution.py:49
  (9 shorter events, 0.0 us)
Async XLA Ops:
  7.2 25.9 %all-gather.4.cloned.1.call-start = ((), (), s32[]{:S(2)}) async-start(), calls=%async_computation.2 | async-start | bytes 1179648 | tf_op jit(solution)/shard_map/all_gather | solution.py:19
  7.9 80.6 %all-gather.6.cloned.1.call-start = ((), (), s32[]{:S(2)}) async-start(), calls=%async_computation.4 | async-start | bytes 1081344 | tf_op jit(solution)/shard_map/all_gather | solution.py:34
  8.6 111.0 %reduce-scatter.2.cloned.1.call-start = ((), (), s32[]{:S(2)}) async-start(), calls=%async_computation.3 | async-start | bytes 1310720 | tf_op jit(solution)/shard_map/reduce_scatter | solution.py:21
  42.5 77.2 %copy-start.1 = (bf16[32,2048]{1,0:T(8,128)(2,1)S(1)}, bf16[32,2048]{1,0:T(8,128)(2,1)}, u32[]{:S(2)}) copy-start(bf16[32,2048]{1,0:T(8,128)(2,1)} %param.9) | copy-start | bytes 393220
  42.5 90.9 %dynamic-slice-start = ((f32[16384]{0:T(1024)}, s32[]{:T(128)}), f32[2048]{0:T(1024)S(1)}, s32[]{:S(2)}) async-start(f32[16384]{0:T(1024)} %param.10, s32[]{:T(128)} %select_n.3), calls=%async_computation.5 | async-start | bytes 16896 | tf_op jit(solution)/shard_map/dynamic_slice | solution.py:29
  89.8 53.2 %copy-start.2 = (f32[4096]{0:T(1024)S(1)}, f32[4096]{0:T(1024)}, u32[]{:S(2)}) copy-start(f32[4096]{0:T(1024)} %param.12) | copy-start | bytes 49156
  135.2 7.8 %all-to-all-start = ((bf16[32,4,512]{2,0,1:T(8,128)(2,1)}), bf16[32,4,512]{2,0,1:T(8,128)(2,1)S(1)}, u32[]{:S(2)}, u32[]{:S(2)}) async-start(bf16[32,4,512]{2,0,1:T(8,128)(2,1)} %bitcast.11), calls=%async_computation.1 | async-start | bytes 262144 | tf_op jit(solution)/shard_map/all_to_all | solution.py:33
  143.0 3.8 %copy-start = (bf16[4096,512]{1,0:T(8,128)(2,1)S(1)}, bf16[4096,512]{1,0:T(8,128)(2,1)}, u32[]{:S(2)}) copy-start(bf16[4096,512]{1,0:T(8,128)(2,1)} %param.13) | copy-start | bytes 12582916
Sparse Core Ops, SparseCore 0:
  9.6 23.4 all-gather.3
  36.1 52.4 all-gather.5
  92.0 27.6 reduce-scatter.1
where the time goes:
time: 206 us; the launch traced here: 205 us
  waiting for transfers between devices  105 us (51%)
  blocking collectives  56.6 us (27%)
  matrix products  19.4 us (9%)
  between operations  15.6 us (8%)
  starting transfers between devices  3.99 us (2%)
  other arithmetic  2.4 us (1%)
    all_gather x1, waiting for transfers between devices, per_device(): lax.all_gather(student_hidden, ('row', 'col'), axis=0, tiled=True)  46 us
    psum x1, blocking collectives, per_device(): grad_gain = lax.psum(gain_part, ('row', 'col'))  43.9 us
    reduce_scatter x1, waiting for transfers between devices, per_device(): lax.psum_scatter(jnp.dot(context_all, out_weight, preferred_element_type=...  29.6 us
    all_gather x1, waiting for transfers between devices, per_device(): context_all = lax.all_gather(context, 'row', axis=0, tiled=True)  24.4 us
    psum x1, blocking collectives, per_device(): squares = lax.psum(jnp.sum(summed * summed, axis=1), 'row')  12.7 us
    dot_general x1, matrix products, per_device(): jnp.dot(context_all, out_weight, preferred_element_type=jnp.float32)  9.41 us
    dot_general x1, matrix products, per_device(): lax.dot_general(student_all, error_term, (((0,), (0,)), ((), ())), prefer...  4.77 us
  transfers between devices with their start and end apart: 4, of which 4 were waited for; matrix products, arithmetic and copies ran while one was open for 5% of the time, Pallas kernels for 0%

commit v1 on v0

--- a/solution.py
+++ b/solution.py
@@ -46,7 +46,8 @@
         error_term, projector, (((1,), (1,)), ((), ())), preferred_element_type=jnp.float32
     )
     gain_part = jnp.sum(grad_normed * normed_all, axis=0)
-    grad_gain = lax.psum(gain_part, ("row", "col"))
+    enter_turns_here = lambda xs, chip_axis, axis_tag: lax.psum(lax.psum(xs, chip_axis), axis_tag)
+    grad_gain = enter_turns_here(gain_part, "col", "row")
     tokens_all = predicted.shape[0]
     loss = loss_total / (tokens_all * D_T)
     return (grad_proj, grad_gain, loss)

time: 206 us -> 247 us (1.20)
  the two profiles are of different devices: /device:TPU:12 before, /device:TPU:0 now
where the time goes in v1:
time: 247 us
  waiting for transfers between devices  108 us (44%)
  blocking collectives  96.1 us (39%)
  matrix products  19.4 us (8%)
  between operations  15.6 us (6%)
  starting transfers between devices  3.44 us (1%)
    all_gather x1, waiting for transfers between devices, per_device(): lax.all_gather(student_hidden, ('row', 'col'), axis=0, tiled=True)  46.8 us
    psum x1, blocking collectives, per_device(): loss_total = lax.psum(loss_part, ('row', 'col'))  37 us
    reduce_scatter x1, waiting for transfers between devices, per_device(): lax.psum_scatter(jnp.dot(context_all, out_weight, preferred_element_type=...  28.9 us
    psum x1, blocking collectives, per_device(): lax.psum(lax.psum(xs, chip_axis), axis_tag)  26.5 us
    all_gather x1, waiting for transfers between devices, per_device(): context_all = lax.all_gather(context, 'row', axis=0, tiled=True)  25.9 us
    psum x1, blocking collectives, per_device(): lax.psum(xs, chip_axis)  16.4 us
    psum x1, blocking collectives, per_device(): squares = lax.psum(jnp.sum(summed * summed, axis=1), 'row')  16.2 us
    dot_general x1, matrix products, per_device(): jnp.dot(context_all, out_weight, preferred_element_type=jnp.float32)  9.41 us
  transfers between devices with their start and end apart: 4, of which 4 were waited for; matrix products, arithmetic and copies ran while one was open for 4% of the time, Pallas kernels for 0%

profile of v1, /device:TPU:0, one launch (start us, length us, event | category | flops | bytes accessed | tf_op | source)
XLA Modules:
  0.0 246.9 jit_solution(8663760593872334987)
XLA Ops:
  7.2 0.0 all-gather.4.cloned.1.call-start
  7.2 0.7 all-gather.4.cloned.1.call-update
  7.9 0.0 all-gather.6.cloned.1.call-start
  7.9 0.7 all-gather.6.cloned.1.call-update
  8.6 0.0 reduce-scatter.2.cloned.1.call-start
  8.7 25.9 %all-gather.4.cloned.1.call-done = bf16[128,4096]{1,0:T(8,128)(2,1)} async-done(((bf16[16,4096]{1,0:T(8,128)(2,1)}), bf16[128,4096]{1,0:T(8,128)(2,1)}) %all-gather.4.cloned.1.call-update) | async-done | bytes 1048592 | tf_op jit(solution)/shard_map/all_gather | solution.py:19
  34.6 9.4 %fusion.4 = f32[128,2048]{1,0:T(8,128)} fusion(bf16[128,4096]{1,0:T(8,128)(2,1)} %all-gather.4.cloned.1.call-done, bf16[4096,2048]{1,0:T(8,128)(2,1)} %param.8), kind=kOutput, calls=%fused_computation.16 | convolution fusion | flops 2147483648 | bytes 18874368 | tf_op jit(solution)/shard_map/dot_general | solution.py:22
  44.0 0.0 reduce-scatter.2.cloned.1.call-update
  44.0 46.8 %all-gather.6.cloned.1.call-done = bf16[32,4,4096]{2,1,0:T(4,128)(2,1)} async-done(((bf16[1,4,4096]{2,1,0:T(4,128)(2,1)}), bf16[32,4,4096]{2,1,0:T(4,128)(2,1)}) %all-gather.6.cloned.1.call-update) | async-done | bytes 1048592 | tf_op jit(solution)/shard_map/all_gather | solution.py:34
  90.9 1.3 reshape.25
  92.2 0.2 multiply_reduce_fusion
  92.4 28.9 %reduce-scatter.2.cloned.1.call-done = f32[32,2048]{1,0:T(8,128)} async-done(((f32[128,2048]{1,0:T(8,128)}), f32[32,2048]{1,0:T(8,128)}) %reduce-scatter.2.cloned.1.call-update) | async-done | bytes 262160 | tf_op jit(solution)/shard_map/reduce_scatter | solution.py:21
  121.3 1.1 multiply_reduce_fusion.2
  122.4 16.2 %psum.28 = f32[32]{0:T(128)S(1)} all-reduce(f32[32]{0:T(128)S(1)} %multiply_reduce_fusion.2), channel_id=1, replica_groups=mesh['row'=8,'col'=4] {'row'}, use_global_device_ids=true, to_apply=%region_3.0 | all-reduce | flops 32 | bytes 256 | tf_op jit(solution)/shard_map/psum | solution.py:28
  138.6 1.0 multiply_convert_fusion.2
  139.6 0.7 copy.14
  140.3 3.3 %all-to-all-start = ((bf16[32,4,512]{2,0,1:T(8,128)(2,1)}), bf16[32,4,512]{2,0,1:T(8,128)(2,1)S(1)}, u32[]{:S(2)}, u32[]{:S(2)}) async-start(bf16[32,4,512]{2,0,1:T(8,128)(2,1)} %bitcast.11), calls=%async_computation.1 | async-start | bytes 262144 | tf_op jit(solution)/shard_map/all_to_all | solution.py:33
  143.7 5.0 %all-to-all-done = bf16[32,4,512]{2,0,1:T(8,128)(2,1)S(1)} async-done(((bf16[32,4,512]{2,0,1:T(8,128)(2,1)}), bf16[32,4,512]{2,0,1:T(8,128)(2,1)S(1)}, u32[]{:S(2)}, u32[]{:S(2)}) %all-to-all-start) | async-done | bytes 131104 | tf_op jit(solution)/shard_map/all_to_all | solution.py:33
  148.7 3.7 %multiply_reduce_fusion.1 = (f32[]{:T(128)}, f32[128,512]{1,0:T(8,128)S(1)}) fusion(f32[128,512]{1,0:T(8,128)S(1)} %bitcast.12, bf16[4096,512]{1,0:T(8,128)(2,1)} %param.13, f32[128,4096]{1,0:T(8,128)S(1)} %reshape.25, f32[4096]{0:T(1024)S(1)} %copy-done.2, f32[128]{0:T(128)S(1)} %add_rsqrt_fusion.1), kind=kOutput, calls=%fused_computation.5 | convolution fusion | flops 538640384 | bytes 6832644 | tf_op jit(solution)/shard_map/dot_general | solution.py:37
  152.4 1.5 fusion
  153.9 4.8 %fusion.1 = f32[4096,512]{1,0:T(8,128)} fusion(f32[128,512]{1,0:T(8,128)S(1)} %get-tuple-element.4, f32[128,4096]{1,0:T(8,128)S(1)} %reshape.25, f32[4096]{0:T(1024)S(1)} %copy-done.2, f32[128]{0:T(128)S(1)} %add_rsqrt_fusion.1), kind=kOutput, calls=%fused_computation.11 | convolution fusion | flops 538574848 | bytes 10764800 | tf_op jit(solution)/shard_map/dot_general | solution.py:42
  158.7 37.0 %psum.31 = f32[]{:T(128)} all-reduce(f32[]{:T(128)} %get-tuple-element.3), channel_id=1, replica_groups=mesh['row'=8,'col'=4] {'row','col'}, use_global_device_ids=true, to_apply=%region_8.0 | all-reduce | flops 1 | bytes 8 | tf_op jit(solution)/shard_map/psum | solution.py:40
  195.7 16.4 %psum.29 = f32[4096]{0:T(1024)S(1)} all-reduce(f32[4096]{0:T(1024)S(1)} %fusion), channel_id=1, replica_groups=mesh['row'=8,'col'=4] {'col'}, use_global_device_ids=true, to_apply=%region_5.0 | all-reduce | flops 4096 | bytes 32768 | tf_op jit(solution)/shard_map/psum | solution.py:49
  212.1 26.5 %psum.30 = f32[4096]{0:T(1024)} all-reduce(f32[4096]{0:T(1024)S(1)} %psum.29), channel_id=1, replica_groups=mesh['row'=8,'col'=4] {'row'}, use_global_device_ids=true, to_apply=%region_6.0 | all-reduce | flops 4096 | bytes 32768 | tf_op jit(solution)/shard_map/psum | solution.py:49
  (11 shorter events, 0.1 us)
Async XLA Ops:
  7.2 27.4 %all-gather.4.cloned.1.call-start = ((), (), s32[]{:S(2)}) async-start(), calls=%async_computation.2 | async-start | bytes 1179648 | tf_op jit(solution)/shard_map/all_gather | solution.py:19
  7.9 83.0 %all-gather.6.cloned.1.call-start = ((), (), s32[]{:S(2)}) async-start(), calls=%async_computation.4 | async-start | bytes 1081344 | tf_op jit(solution)/shard_map/all_gather | solution.py:34
  8.6 112.7 %reduce-scatter.2.cloned.1.call-start = ((), (), s32[]{:S(2)}) async-start(), calls=%async_computation.3 | async-start | bytes 1310720 | tf_op jit(solution)/shard_map/reduce_scatter | solution.py:21
  44.0 77.3 %copy-start.1 = (bf16[32,2048]{1,0:T(8,128)(2,1)S(1)}, bf16[32,2048]{1,0:T(8,128)(2,1)}, u32[]{:S(2)}) copy-start(bf16[32,2048]{1,0:T(8,128)(2,1)} %param.9) | copy-start | bytes 393220
  44.0 94.6 %dynamic-slice-start = ((f32[16384]{0:T(1024)}, s32[]{:T(128)}), f32[2048]{0:T(1024)S(1)}, s32[]{:S(2)}) async-start(f32[16384]{0:T(1024)} %param.10, s32[]{:T(128)} %select_n.3), calls=%async_computation.5 | async-start | bytes 16896 | tf_op jit(solution)/shard_map/dynamic_slice | solution.py:29
  92.2 56.5 %copy-start.2 = (f32[4096]{0:T(1024)S(1)}, f32[4096]{0:T(1024)}, u32[]{:S(2)}) copy-start(f32[4096]{0:T(1024)} %param.12) | copy-start | bytes 49156
  140.3 8.3 %all-to-all-start = ((bf16[32,4,512]{2,0,1:T(8,128)(2,1)}), bf16[32,4,512]{2,0,1:T(8,128)(2,1)S(1)}, u32[]{:S(2)}, u32[]{:S(2)}) async-start(bf16[32,4,512]{2,0,1:T(8,128)(2,1)} %bitcast.11), calls=%async_computation.1 | async-start | bytes 262144 | tf_op jit(solution)/shard_map/all_to_all | solution.py:33
  148.7 3.8 %copy-start = (bf16[4096,512]{1,0:T(8,128)(2,1)S(1)}, bf16[4096,512]{1,0:T(8,128)(2,1)}, u32[]{:S(2)}) copy-start(bf16[4096,512]{1,0:T(8,128)(2,1)} %param.13) | copy-start | bytes 12582916
Sparse Core Ops, SparseCore 0:
  9.6 24.9 all-gather.3
  37.6 53.2 all-gather.5
  94.3 26.9 reduce-scatter.1
